TPU v7x, 32 devices: a whole 2x2x4 slice. The times are simulated.
32 devices in a mesh: fsdp: 8 (over z, x), rep: 4 (over y, core).
Axes of the slice: x: 2, y: 2, z: 4, core: 2. Of those that a mesh axis runs over, the one named last changes fastest.
Arguments:
- hidden_in: bfloat16 [16384, 768], P(('fsdp', 'rep')), may hold values from -6 to 6
- cotangent: bfloat16 [16384, 768], P(('fsdp', 'rep')), may hold values from -6 to 6
- lengths: int32 [32], P(('fsdp', 'rep')), may hold values from 1 to 512, as said below
- norm_gain: bfloat16 [768], P('fsdp'), may hold values from 0.5 to 1.5
- in_weight: bfloat16 [768, 3352], P('fsdp'), may hold values from -0.21875 to 0.21875
- conv_weight: bfloat16 [4, 1792], P(None, 'fsdp'), may hold values from -3 to 3
- conv_bias: bfloat16 [1792], P('fsdp'), may hold values from -2 to 2
- step_bias: float32 [24], replicated, may hold values from -6 to -2
- decay_log: float32 [24], replicated, may hold values from 0 to 2.77
- skip_weight: float32 [24], replicated, may hold values from 0.5 to 1.5
- mix_gain: bfloat16 [1536], P('fsdp'), may hold values from 0.5 to 1.5
- out_weight: bfloat16 [1536, 768], P('fsdp'), may hold values from -0.15625 to 0.15625
Outputs:
- block_out: bfloat16 [16384, 768], P(('fsdp', 'rep'))
- grad_in: float32 [16384, 768], P(('fsdp', 'rep'))
- grad_norm_gain: float32 [768], P('fsdp')
- grad_in_weight: float32 [768, 3352], P('fsdp')
- grad_conv_weight: float32 [4, 1792], P(None, 'fsdp')
- grad_conv_bias: float32 [1792], P('fsdp')
- grad_step_bias: float32 [24], replicated
- grad_decay_log: float32 [24], replicated
- grad_skip_weight: float32 [24], replicated
- grad_mix_gain: float32 [1536], P('fsdp')
- grad_out_weight: float32 [1536, 768], P('fsdp')
Inputs may be any that keep to these rules, and one draw needn't show every extreme that they name: lengths[s] is the number of live tokens of sequence s, which fill its first slots; some sequence has 512 live tokens.
All inputs are finite; a program needn't handle non-finite values.
Results may differ from a plain program's by a relative error of at most 0.0068.
Values may be sent and summed in bfloat16 or wider, within the bound.
A program may use at most 192 MiB of HBM per device.

v0:
```python
import functools


import jax
import jax.numpy as jnp
from jax import lax
from jax.experimental import pallas as pl
from jax.experimental.pallas import tpu as pltpu
from jax.sharding import PartitionSpec as P

NH = 24
HD = 64
NS = 128
KCONV = 4
DI = 1536
CONV_CH = 1792
PROJ = 3352
LANES = 128
PAIR = LANES // HD
CUTS = (0, 1152, 2304, PROJ)

EPS = 1e-05
HIGH = lax.Precision.HIGHEST


def pre_norm(rows, gain):
    scale = lax.rsqrt(jnp.mean(rows * rows, axis=-1, keepdims=True) + EPS)
    return rows * scale * gain


def contract(left, right, left_dim, right_dim, precision=None):
    return lax.dot_general(
        left,
        right,
        (((left_dim,), (right_dim,)), ((), ())),
        precision=precision,
        preferred_element_type=jnp.float32,
    )


def column_of(array, head):
    lane = lax.broadcasted_iota(jnp.int32, array.shape, 1)
    return jnp.sum(jnp.where(lane == head, array, 0.0), axis=1, keepdims=True)


def tiles_of(length):
    half = length // 2
    return half, ((0, 0), (1, 0), (1, 1))


def decay_tile(cum_col, cum_row, half, row, col):
    spread = cum_col[row * half : (row + 1) * half] - cum_row[:, col * half : (col + 1) * half]
    if row == col:
        rows = lax.broadcasted_iota(jnp.int32, spread.shape, 0)
        cols = lax.broadcasted_iota(jnp.int32, spread.shape, 1)
        spread = jnp.where(rows >= cols, spread, -jnp.inf)
    return jnp.exp(spread)


def pair_lanes(shape):
    return lax.broadcasted_iota(jnp.int32, shape, 1) // HD


def scan_fwd_kernel(x_ref, dt_ref, cum_ref, cumt_ref, b_ref, c_ref, y_ref, score):
    pair = pl.program_id(0)
    length = x_ref.shape[0]
    half, tiles = tiles_of(length)

    @pl.when(pair == 0)
    def _():
        score[...] = contract(c_ref[...], b_ref[...], 1, 1, HIGH)

    which = pair_lanes(x_ref.shape)
    x = x_ref[...]
    sums = [None, None]
    for sub in range(PAIR):
        head = pair * PAIR + sub
        cum_col = column_of(cum_ref[...], head)
        cum_row = cumt_ref[pl.ds(head, 1), :]
        scaled = jnp.where(which == sub, x * column_of(dt_ref[...], head), 0.0)
        scaled = scaled.astype(jnp.bfloat16)
        for row, col in tiles:
            decay = decay_tile(cum_col, cum_row, half, row, col)
            part = score[row * half : (row + 1) * half, col * half : (col + 1) * half]
            mixed = (part * decay).astype(jnp.bfloat16)
            term = contract(mixed, scaled[col * half : (col + 1) * half], 1, 0)
            sums[row] = term if sums[row] is None else sums[row] + term
    for row in range(2):
        y_ref[row * half : (row + 1) * half, :] = sums[row]


def scan_bwd_kernel(
    x_ref, dt_ref, cum_ref, cumt_ref, b_ref, c_ref, dy_ref,
    dx_ref, ddt_ref, drow_ref, dcol_ref, db_ref, dc_ref, score, dscore,
):
    pair = pl.program_id(0)
    length = x_ref.shape[0]
    half, tiles = tiles_of(length)

    @pl.when(pair == 0)
    def _():
        score[...] = contract(c_ref[...], b_ref[...], 1, 1, HIGH)
        dscore[...] = jnp.zeros_like(dscore)
        ddt_ref[...] = jnp.zeros_like(ddt_ref)
        drow_ref[...] = jnp.zeros_like(drow_ref)

    which = pair_lanes(x_ref.shape)
    lane = lax.broadcasted_iota(jnp.int32, x_ref.shape, 1)
    x = x_ref[...]
    dy = dy_ref[...]
    d_scaled = [None, None]
    dt_pair = jnp.zeros_like(x)
    for sub in range(PAIR):
        head = pair * PAIR + sub
        cum_col = column_of(cum_ref[...], head)
        cum_row = cumt_ref[pl.ds(head, 1), :]
        dt_here = jnp.where(which == sub, column_of(dt_ref[...], head), 0.0)
        dt_pair = dt_pair + dt_here
        scaled = (x * dt_here).astype(jnp.bfloat16)
        dy_here = jnp.where(which == sub, dy, 0.0).astype(jnp.bfloat16)
        row_sum = [None, None]
        col_sum = [None, None]
        for row, col in tiles:
            rows = slice(row * half, (row + 1) * half)
            cols = slice(col * half, (col + 1) * half)
            decay = decay_tile(cum_col, cum_row, half, row, col)
            part = score[rows, cols]
            mixed = (part * decay).astype(jnp.bfloat16)
            d_mixed = contract(dy_here[rows], scaled[cols], 1, 1) * decay
            dscore[rows, cols] += d_mixed
            weight = d_mixed * part
            over_cols = jnp.sum(weight, axis=1, keepdims=True)
            over_rows = jnp.sum(weight, axis=0, keepdims=True)
            term = contract(mixed, dy_here[rows], 0, 0)
            row_sum[row] = over_cols if row_sum[row] is None else row_sum[row] + over_cols
            col_sum[col] = over_rows if col_sum[col] is None else col_sum[col] + over_rows
            d_scaled[col] = term if d_scaled[col] is None else d_scaled[col] + term
        for part_index in range(2):
            span = slice(part_index * half, (part_index + 1) * half)
            drow_ref[span, :] = jnp.where(lane[span] == head, row_sum[part_index], drow_ref[span, :])
            dcol_ref[pl.ds(head, 1), span] = col_sum[part_index]
    for part_index in range(2):
        span = slice(part_index * half, (part_index + 1) * half)
        dx_ref[span, :] = d_scaled[part_index] * dt_pair[span]
        products = d_scaled[part_index] * x[span]
        for sub in range(PAIR):
            head = pair * PAIR + sub
            total = jnp.sum(
                jnp.where(which[span] == sub, products, 0.0), axis=1, keepdims=True
            )
            ddt_ref[span, :] = jnp.where(lane[span] == head, total, ddt_ref[span, :])

    @pl.when(pair == pl.num_programs(0) - 1)
    def _():
        dc_ref[...] = contract(dscore[...], b_ref[...], 1, 0, HIGH)
        db_ref[...] = contract(dscore[...], c_ref[...], 0, 0, HIGH)


def whole_spec(shape):
    return pl.BlockSpec(shape, lambda pair: (0, 0))


def scan_operands(x, dt, cum):
    pad = ((0, 0), (0, LANES - NH))
    return x, jnp.pad(dt, pad), jnp.pad(cum, pad), cum.T


def scan_specs(length):
    lanes = whole_spec((length, LANES))
    return [
        pl.BlockSpec((length, LANES), lambda pair: (0, pair)),
        lanes,
        lanes,
        whole_spec((NH, length)),
        whole_spec((length, NS)),
        whole_spec((length, NS)),
    ]


@jax.custom_vjp
def span_scan(x, dt, cum, keys_b, query_c):
    length = x.shape[0]
    return pl.pallas_call(
        scan_fwd_kernel,
        grid=(NH // PAIR,),
        in_specs=scan_specs(length),
        out_specs=pl.BlockSpec((length, LANES), lambda pair: (0, pair)),
        out_shape=jax.ShapeDtypeStruct(x.shape, jnp.float32),
        scratch_shapes=[pltpu.VMEM((length, length), jnp.float32)],
        name="scan_fwd",
    )(*scan_operands(x, dt, cum), keys_b, query_c)


def span_scan_fwd(x, dt, cum, keys_b, query_c):
    return span_scan(x, dt, cum, keys_b, query_c), (x, dt, cum, keys_b, query_c)


def span_scan_bwd(saved, dy):
    x, dt, cum, keys_b, query_c = saved
    length = x.shape[0]
    pair_block = pl.BlockSpec((length, LANES), lambda pair: (0, pair))
    lanes = whole_spec((length, LANES))
    square = pltpu.VMEM((length, length), jnp.float32)
    f32 = jnp.float32
    dx, ddt, drow, dcol, db, dc = pl.pallas_call(
        scan_bwd_kernel,
        grid=(NH // PAIR,),
        in_specs=scan_specs(length) + [pair_block],
        out_specs=[
            pair_block, lanes, lanes, whole_spec((NH, length)),
            whole_spec((length, NS)), whole_spec((length, NS)),
        ],
        out_shape=[
            jax.ShapeDtypeStruct(x.shape, f32),
            jax.ShapeDtypeStruct((length, LANES), f32),
            jax.ShapeDtypeStruct((length, LANES), f32),
            jax.ShapeDtypeStruct((NH, length), f32),
            jax.ShapeDtypeStruct((length, NS), f32),
            jax.ShapeDtypeStruct((length, NS), f32),
        ],
        scratch_shapes=[square, square],
        name="scan_bwd",
    )(*scan_operands(x, dt, cum), keys_b, query_c, dy)
    return dx, ddt[:, :NH], drow[:, :NH] - dcol.T, db, dc


span_scan.defvjp(span_scan_fwd, span_scan_bwd)


def mixer_core(proj, conv_w, conv_b, step_bias, decay_log, skip_weight, mix_gain):
    length = proj.shape[0]
    gate = proj[:, :DI]
    conv_in = proj[:, DI : DI + CONV_CH]
    step_raw = proj[:, DI + CONV_CH :]
    padded = jnp.pad(conv_in, ((KCONV - 1, 0), (0, 0)))
    conv_out = jnp.zeros_like(conv_in) + conv_b
    for offset in range(KCONV):
        conv_out = conv_out + conv_w[offset] * padded[offset : offset + length]
    active = jax.nn.silu(conv_out)
    values = active[:, :DI]
    keys_b = active[:, DI : DI + NS]
    query_c = active[:, DI + NS :]
    step = jax.nn.softplus(step_raw + step_bias)
    logdecay = -step * jnp.exp(decay_log)
    causal = (jnp.arange(length)[:, None] >= jnp.arange(length)[None, :]).astype(jnp.float32)
    cum = jnp.dot(causal, logdecay, precision=HIGH)
    mixed = span_scan(values, step, cum, keys_b, query_c)
    mixed = mixed + jnp.repeat(skip_weight, HD) * values
    flat = mixed * jax.nn.silu(gate)
    scale = lax.rsqrt(jnp.mean(flat * flat, axis=-1, keepdims=True) + EPS)
    return flat * scale * mix_gain


def bits_of(axis):
    size = lax.axis_size(axis)
    return [(axis, 1 << k) for k in reversed(range(size.bit_length() - 1))]


def all_labels():
    return bits_of("fsdp") + bits_of("rep")


def my_bit(label):
    return (lax.axis_index(label[0]) // label[1]) % 2


def partner(label):
    ids = {name: lax.axis_index(name) for name in ("fsdp", "rep")}
    ids[label[0]] = ids[label[0]] + label[1] * (1 - 2 * my_bit(label))
    return (ids["fsdp"], ids["rep"])


def greet(labels):
    barrier = pltpu.get_barrier_semaphore()
    for label in labels:
        pl.semaphore_signal(
            barrier, inc=1, device_id=partner(label), device_id_type=pl.DeviceIdType.MESH
        )
    pl.semaphore_wait(barrier, len(labels))


def send(source, target, sems, stream, slot, label):
    copy = pltpu.make_async_remote_copy(
        src_ref=source,
        dst_ref=target,
        send_sem=sems[0].at[stream, slot],
        recv_sem=sems[1].at[stream, slot],
        device_id=partner(label),
        device_id_type=pl.DeviceIdType.MESH,
    )
    copy.start()
    return copy


def orders():
    fsdp, rep = bits_of("fsdp"), bits_of("rep")
    near, wide = fsdp[-1:], fsdp[:-1]
    mid, far = wide[-1:], wide[:-1]
    core, row = rep[-1:], rep[:-1]
    return (
        core + row + near + mid + far,
        core + near + mid + row + far,
        core + mid + row + near + far,
    )


def position(order):
    place = 0
    for label in order:
        place = place * 2 + my_bit(label)
    return place


def gather_kernel(plan, *refs):
    count = len(plan)
    ins, outs = refs[:count], refs[count : 2 * count]
    sems, local = refs[2 * count : 2 * count + 2], refs[2 * count + 2]
    greet(all_labels())
    steps = max(len(order) for order in plan)
    open_sends, waiting, locals_ = [], {}, []
    for k in range(count):
        copy = pltpu.make_async_copy(ins[k], outs[k].at[pl.ds(position(plan[k]), 1)], local.at[k])
        copy.start()
        locals_.append(copy)
    for step in range(steps):
        for k, order in enumerate(plan):
            if step >= len(order):
                continue
            size = 1 << step
            start = position(order) // size * size
            if step == 0:
                source = ins[k]
            else:
                if step == 1:
                    locals_[k].wait()
                waiting[k].wait_recv()
                source = outs[k].at[pl.ds(start, size)]
            label = order[len(order) - 1 - step]
            copy = send(source, outs[k].at[pl.ds(start, size)], sems, k, step, label)
            waiting[k] = copy
            open_sends.append(copy)
    for k in range(count):
        waiting[k].wait_recv()
        if len(plan[k]) < 2:
            locals_[k].wait()
    for copy in open_sends:
        copy.wait_send()


def gather_all(plan, pieces):
    steps = max(len(order) for order in plan)
    vmem = pl.BlockSpec(memory_space=pltpu.VMEM)
    return pl.pallas_call(
        functools.partial(gather_kernel, plan),
        in_specs=[vmem] * len(pieces),
        out_specs=[vmem] * len(pieces),
        out_shape=[
            jax.ShapeDtypeStruct((1 << len(order),) + piece.shape[1:], piece.dtype)
            for order, piece in zip(plan, pieces)
        ],
        scratch_shapes=[
            pltpu.SemaphoreType.DMA((len(pieces), steps)),
            pltpu.SemaphoreType.DMA((len(pieces), steps)),
            pltpu.SemaphoreType.DMA((len(pieces),)),
        ],
        compiler_params=pltpu.CompilerParams(
            collective_id=0, has_side_effects=True, vmem_limit_bytes=60 << 20
        ),
        name="gather_weights",
    )(*pieces)


def reduce_kernel(plan, tail, *refs):
    count = len(plan)
    steps = len(plan[0])
    grads, vector = refs[:count], refs[count]
    outs, total = refs[count + 1 : 2 * count + 1], refs[2 * count + 1]
    at = 2 * count + 2
    held = [refs[at + k * steps : at + (k + 1) * steps] for k in range(count)]
    at += count * steps
    sums = refs[at : at + steps]
    sems, local = refs[at + steps : at + steps + 2], refs[at + steps + 2]
    labels = all_labels()
    greet(labels)
    open_sends, waiting = [], {}
    vector_order = labels[::-1]

    def source_of(k, step):
        return grads[k] if step == 0 else held[k][step - 1]

    def add_in(k, step):
        size = 1 << (steps - 1 - step)
        base = source_of(k, step)
        target = held[k][step]
        start = my_bit(plan[k][step]) * size

        def one(i, carry):
            left = base[start + i].astype(jnp.float32)
            target[i] = (left + target[i].astype(jnp.float32)).astype(target.dtype)
            return carry

        lax.fori_loop(0, size, one, 0)

    for step in range(steps):
        for k in range(count):
            if step > 0:
                waiting[k].wait_recv()
                add_in(k, step - 1)
            label = plan[k][step]
            size = 1 << (steps - 1 - step)
            away = source_of(k, step).at[pl.ds((1 - my_bit(label)) * size, size)]
            waiting[k] = send(away, held[k][step], sems, k, step, label)
            open_sends.append(waiting[k])
        if step > 0:
            waiting[count].wait_recv()
            before = vector if step == 1 else sums[step - 2]
            sums[step - 1][...] = before[...] + sums[step - 1][...]
        now = vector if step == 0 else sums[step - 1]
        waiting[count] = send(now, sums[step], sems, count, step, vector_order[step])
        open_sends.append(waiting[count])

    here = lax.axis_index("rep")
    known = {k: [0] for k in range(count)}
    inbox = {k: [] for k in range(count)}
    for hop, label in enumerate(tail):
        for k in range(count):
            if hop == 0:
                waiting[k].wait_recv()
                add_in(k, steps - 1)
                copy = pltpu.make_async_copy(
                    held[k][steps - 1], outs[k].at[pl.ds(here, 1)], local.at[k]
                )
                copy.start()
                waiting[k] = copy
            for copy in inbox[k]:
                copy.wait_recv()
            inbox[k] = []
            shift = label[1] * (1 - 2 * my_bit(label))
            for n, offset in enumerate(list(known[k])):
                place = pl.ds(here + offset, 1)
                source = held[k][steps - 1] if n == 0 else outs[k].at[place]
                copy = send(source, outs[k].at[place], sems, k, steps + (1 << hop) - 1 + n, label)
                inbox[k].append(copy)
                open_sends.append(copy)
                known[k].append(offset + shift)
    waiting[count].wait_recv()
    before = sums[steps - 2]
    total[...] = before[...] + sums[steps - 1][...]
    for k in range(count):
        for copy in inbox[k]:
            copy.wait_recv()
        waiting[k].wait()
    for copy in open_sends:
        copy.wait_send()


def reduce_all(plan, grads, vector):
    steps = len(plan[0])
    reps = lax.axis_size("rep")
    vmem = pl.BlockSpec(memory_space=pltpu.VMEM)
    slots = pltpu.SemaphoreType.DMA((len(grads) + 1, steps + reps))
    scratch = []
    for grad in grads:
        scratch += [
            pltpu.VMEM((1 << (steps - 1 - step),) + grad.shape[1:], grad.dtype)
            for step in range(steps)
        ]
    scratch += [pltpu.VMEM(vector.shape, vector.dtype) for _ in range(steps)]
    return pl.pallas_call(
        functools.partial(reduce_kernel, plan, bits_of("rep")),
        in_specs=[vmem] * (len(grads) + 1),
        out_specs=[vmem] * (len(grads) + 1),
        out_shape=[jax.ShapeDtypeStruct((reps,) + g.shape[1:], g.dtype) for g in grads]
        + [jax.ShapeDtypeStruct(vector.shape, vector.dtype)],
        scratch_shapes=scratch + [slots, slots, pltpu.SemaphoreType.DMA((len(grads),))],
        compiler_params=pltpu.CompilerParams(
            collective_id=1, has_side_effects=True, vmem_limit_bytes=60 << 20
        ),
        name="reduce_grads",
    )(*grads, vector)


def to_order(array, order):
    labels = all_labels()
    rows = array.shape[0] >> len(labels)
    perm = [labels.index(label) for label in order] + [len(labels), len(labels) + 1]
    split = array.reshape((2,) * len(labels) + (rows, array.shape[1]))
    return split.transpose(perm).reshape((-1, rows, array.shape[1]))


def from_order(blocks, order):
    labels = all_labels()
    perm = [order.index(label) for label in labels] + [len(labels), len(labels) + 1]
    split = blocks.reshape((2,) * len(labels) + blocks.shape[1:])
    return split.transpose(perm).reshape((-1, blocks.shape[-1]))


def my_rows(shard):
    count = shard.shape[0] // lax.axis_size("rep")
    return lax.dynamic_slice_in_dim(shard, lax.axis_index("rep") * count, count, 0)


def body(
    hidden_in, cotangent, lengths, norm_gain, in_weight, conv_weight, conv_bias,
    step_bias, decay_log, skip_weight, mix_gain, out_weight,
):
    plan = orders()
    columns = [slice(CUTS[k], CUTS[k + 1]) for k in range(len(CUTS) - 1)]
    width = out_weight.shape[1] // len(columns)
    out_columns = [slice(k * width, (k + 1) * width) for k in range(len(columns))]
    small = jnp.concatenate([norm_gain, conv_weight.reshape(-1), conv_bias, mix_gain])
    small = jnp.pad(small, (0, -small.size % 2048)).reshape(1, -1, LANES)
    in_rows, out_rows = my_rows(in_weight), my_rows(out_weight)
    pieces = [small] + [in_rows[None, :, cut] for cut in columns]
    pieces += [out_rows[None, :, cut] for cut in out_columns]
    wide_plan = list(plan) + list(plan)
    gathered = gather_all([bits_of("fsdp")] + wide_plan, pieces)
    full = [from_order(blocks, order) for blocks, order in zip(gathered[1:], wide_plan)]
    in_full = jnp.concatenate(full[: len(columns)], axis=1)
    out_full = jnp.concatenate(full[len(columns) :], axis=1)
    small = gathered[0].reshape(lax.axis_size("fsdp"), -1)
    groups = small.shape[0]
    ends = [norm_gain.size, conv_weight.size, conv_bias.size]
    cut_a, cut_b, cut_c = ends[0], ends[0] + ends[1], sum(ends)
    gain_full = small[:, :cut_a].reshape(-1)
    conv_full = small[:, cut_a:cut_b].reshape(groups, KCONV, -1).transpose(1, 0, 2)
    conv_full = conv_full.reshape(KCONV, -1)
    bias_full = small[:, cut_b:cut_c].reshape(-1)
    mix_full = small[:, cut_c : cut_c + mix_gain.size].reshape(-1)

    seq_count = lengths.shape[0]
    rows_here = hidden_in.shape[0]
    length = rows_here // seq_count

    def core(proj, *params):
        parts = [
            mixer_core(proj[s * length : (s + 1) * length], *params) for s in range(seq_count)
        ]
        return parts[0] if seq_count == 1 else jnp.concatenate(parts)

    resid = hidden_in.astype(jnp.float32)
    normed, norm_back = jax.vjp(pre_norm, resid, gain_full.astype(jnp.float32))
    normed_b = normed.astype(jnp.bfloat16)
    proj = jnp.dot(normed_b, in_full, preferred_element_type=jnp.float32)
    gated, core_back = jax.vjp(
        core,
        proj,
        conv_full.astype(jnp.float32),
        bias_full.astype(jnp.float32),
        step_bias,
        decay_log,
        skip_weight,
        mix_full.astype(jnp.float32),
    )
    gated_b = gated.astype(jnp.bfloat16)
    branch = jnp.dot(gated_b, out_full, preferred_element_type=jnp.float32)
    live = (
        (jnp.arange(length)[None, :] < lengths[:, None]).reshape(rows_here, 1).astype(jnp.float32)
    )
    block_out = (resid + live * branch).astype(jnp.bfloat16)
    cot_live = cotangent * live.astype(jnp.bfloat16)
    d_out_w = contract(gated_b, cot_live, 0, 0)
    d_gated = contract(cot_live, out_full, 1, 1)
    d_proj, d_cw, d_cb, d_sb, d_dl, d_sk, d_mg = core_back(d_gated)
    d_proj_b = d_proj.astype(jnp.bfloat16)
    d_normed = contract(d_proj_b, in_full, 1, 1)
    d_resid, d_gain = norm_back(d_normed)
    grad_in = cotangent.astype(jnp.float32) + d_resid

    vectors = [d_gain, d_cw.reshape(-1), d_cb, d_mg, d_sb, d_dl, d_sk]
    packed = jnp.concatenate(vectors)
    packed = jnp.pad(packed, (0, -packed.size % 1024)).reshape(-1, LANES)
    partial = [contract(normed_b, d_proj_b[:, cut], 0, 0) for cut in columns]
    partial += [d_out_w[:, cut] for cut in out_columns]
    blocks = [
        to_order(part.astype(jnp.bfloat16), order) for part, order in zip(partial, wide_plan)
    ]
    *sums, packed = reduce_all(wide_plan, blocks, packed)
    sums = [part.reshape(-1, part.shape[-1]) for part in sums]
    g_in = jnp.concatenate(sums[: len(columns)], axis=1).astype(jnp.float32)
    g_out = jnp.concatenate(sums[len(columns) :], axis=1).astype(jnp.float32)
    packed = packed.reshape(-1)
    totals = []
    at = 0
    for vector in vectors:
        totals.append(packed[at : at + vector.size])
        at += vector.size
    me = lax.axis_index("fsdp")

    def mine(array, dim):
        count = array.shape[dim] // groups
        return lax.dynamic_slice_in_dim(array, me * count, count, dim)

    g_gain = mine(totals[0], 0)
    g_cw = mine(totals[1].reshape(KCONV, -1), 1)
    g_cb = mine(totals[2], 0)
    g_mg = mine(totals[3], 0)
    g_sb, g_dl, g_sk = totals[4:]
    return (block_out, grad_in, g_gain, g_in, g_cw, g_cb, g_sb, g_dl, g_sk, g_mg, g_out)


def solution(mesh):
    in_specs = (
        P(("fsdp", "rep"), None),
        P(("fsdp", "rep"), None),
        P(("fsdp", "rep")),
        P("fsdp"),
        P("fsdp", None),
        P(None, "fsdp"),
        P("fsdp"),
        P(),
        P(),
        P(),
        P("fsdp"),
        P("fsdp", None),
    )
    out_specs = (
        P(("fsdp", "rep"), None),
        P(("fsdp", "rep"), None),
        P("fsdp"),
        P("fsdp", None),
        P(None, "fsdp"),
        P("fsdp"),
        P(),
        P(),
        P(),
        P("fsdp"),
        P("fsdp", None),
    )
    return jax.shard_map(body, mesh=mesh, in_specs=in_specs, out_specs=out_specs, check_vma=False)
```

profile of v0, /device:TPU:0, one launch (start us, length us, event | category | flops | bytes accessed | tf_op | source)
XLA Modules:
  0.0 259.2 jit_solution(8240631741413518095)
XLA Ops:
  1.4 2.1 concatenate.18
  4.1 1.5 dynamic-slice_bitcast_fusion.1
  5.6 1.4 dynamic-slice_bitcast_fusion.refs_3_
  8.4 50.0 %gather_weights.1 = (bf16[8,16,128]{2,1,0:T(8,128)(2,1)}, bf16[32,24,1152]{2,1,0:T(8,128)(2,1)}, bf16[32,24,1152]{2,1,0:T(8,128)(2,1)}, bf16[32,24,1048]{2,1,0:T...) custom-call(bf16[1,16,128]{2,1,0:T(8,128)(2,1)} %pad_bitcast_fusion.1.refs_0_, ...), custom_call_target="tpu_custom_call" | custom-call | tf_op jit(solution)/shard_map/gather_weights/pallas_call | solution.py:353
  58.4 2.2 copy.85
  60.7 2.2 copy.84
  68.7 5.1 %fusion.7 = f32[512,3352]{1,0:T(8,128)S(1)} fusion(bf16[768,1048]{1,0:T(8,128)(2,1)S(1)} %bitcast.103, bf16[768,1152]{1,0:T(8,128)(2,1)} %bitcast.105, bf16[768,1152]{1,0:T(8,128)(2,1)} %bitcast.107, bf16[512,768]{1,0:T(8,128)(2,1)S(1)} %copy-done.9, f32[768]{0:T(1024)S(1)} %reshape.314, f32[512]{0:T(512)S(1)} %fusion.38), kind=kOutput, calls=%fused_computation.42 | convolution fusion | flops 2653138944 | bytes 12805120 | tf_op jit(solution)/shard_map/dot_general | solution.py:544
  73.8 2.3 slice.178
  76.1 1.8 copy-done.5
  78.6 8.4 %fusion.2 = (f32[512,1792]{1,0:T(8,128)S(1)}, f32[512,1792]{1,0:T(8,128)}) fusion(f32[512,1792]{1,0:T(8,128)} %slice.178, f32[1792]{0:T(1024)S(1)} %mul.323, f32[1792]{0:T(1024)S(1)} %mul.320, f32[1792]{0:T(1024)S(1)} %mul.317, f32[1792]{0:T(1024)S(1)} %mul.309, f32[1792]{0:T(1024)S(1)} %reshape.313), kind=kLoop, calls=%fused_computation.15 | loop fusion | flops 11010048 | bytes 11045888 | tf_op jit(solution)/shard_map/jvp(jit(silu))/mul | solution.py:239
  87.0 2.4 slice.182.x_ref
  93.1 1.9 fusion.54
  95.0 12.7 %jvp_scan_fwd_.1 = f32[512,1536]{1,0:T(8,128)} custom-call(f32[512,1536]{1,0:T(8,128)} %slice.182.x_ref, f32[512,128]{1,0:T(8,128)} %pad.70.dt_ref, f32[512,128]{1,0:T(8,128)} %pad.71.cum_ref, f32[24,512]{1,0:T(8,128)} %bitcast.123, f32[512,128]{1,0:T(8,128)} %get-tuple-element.79.b_ref, f32[512,128]{1,0:T(8,128)} %get-tuple-element.78.c_ref), custom_call_target="tpu_custom_call" | custom-call | tf_op jit(solution)/shard_map/jvp(scan_fwd)/pallas_call | solution.py:183
  107.8 4.9 %multiply_reduce_fusion.7 = (f32[512]{0:T(512)S(1)}, f32[512,1536]{1,0:T(8,128)S(1)}) fusion(f32[512,3352]{1,0:T(8,128)} %copy-done.5, f32[512,1536]{1,0:T(8,128)} %jvp_scan_fwd_.1, f32[512,1792]{1,0:T(8,128)} %copy-done, f32[1536]{0:T(1024)S(1)} %mul.329), kind=kLoop, calls=%fused_computation.30 | loop fusion | flops 7077376 | bytes 12591104 | tf_op jit(solution)/shard_map/jvp()/reduce_sum | solution.py:250
  112.9 5.2 %fusion.14 = bf16[512,768]{1,0:T(8,128)(2,1)} fusion(bf16[512,768]{1,0:T(8,128)(2,1)} %param.12, bf16[1536,256]{1,0:T(8,128)(2,1)} %bitcast.114, bf16[1536,256]{1,0:T(8,128)(2,1)} %bitcast.116, bf16[1536,256]{1,0:T(8,128)(2,1)} %bitcast.118, f32[512]{0:T(512)S(1)} %get-tuple-element.94, f32[512,1536]{1,0:T(8,128)S(1)} %get-tuple-element.70, ...), kind=kOutput, calls=%fused_computation.53 | convolution fusion | flops 1218969600 | bytes 7088128 | tf_op jit(solution)/shard_map/dot_general | solution.py:556
  118.1 1.7 multiply_reduce_fusion.5
  121.1 5.8 %multiply_reduce_fusion.4 = (f32[1536]{0:T(1024)S(1)}, f32[512,1536]{1,0:T(8,128)}, f32[512,1536]{1,0:T(8,128)}) fusion(f32[512,1792]{1,0:T(8,128)S(1)} %copy-done.1, f32[512,3352]{1,0:T(8,128)} %copy-done.5, f32[512,1536]{1,0:T(8,128)S(1)} %get-tuple-element.70, f32[512]{0:T(512)S(1)} %multiply_multiply_fusion.1, f32[512]{0:T(512)S(1)} %fusion.39, ...), kind=kLoop, calls=%fused_computation.25 | loop fusion | flops 16513536 | bytes 22042624 | tf_op jit(solution)/shard_map/transpose(jvp())/reduce_sum | solution.py:248
  126.9 22.0 %transpose_jvp_scan_bwd__.1 = (f32[512,1536]{1,0:T(8,128)}, f32[512,128]{1,0:T(8,128)}, f32[512,128]{1,0:T(8,128)}, f32[24,512]{1,0:T(8,128)}, f32[512,128]{1,0:T(8,128)}, /*index=5*/f32[512,128]{1,0:T(8,128)}) custom-call(f32[512,1536]{1,0:T(8,128)} %slice.182.x_ref, f32[512,128]{1,0:T(8,128)} %pad.70.dt_ref, f32[512,128]{1,0:T(8,128)} %pad.71.cum_ref, ...), custom_call_target="tpu_custom_call" | custom-call | tf_op jit(solution)/shard_map/transpose(jvp(scan_bwd))/pallas_call | solution.py:247
  149.0 2.7 %multiply_add_fusion.1 = f32[512,1536]{1,0:T(8,128)S(1)} fusion(f32[512,1536]{1,0:T(8,128)} %get-tuple-element.43, f32[512,1536]{1,0:T(8,128)S(1)} %copy-done.4, f32[1536]{0:T(1024)S(1)} %mul.329), kind=kLoop, calls=%fused_computation.27 | loop fusion | flops 1572864 | bytes 9443328 | tf_op jit(solution)/shard_map/transpose(jvp())/add_any | solution.py:247
  153.1 5.0 %multiply_reduce_fusion.2 = (f32[1792]{0:T(1024)S(1)}, f32[1792]{0:T(1024)S(1)}, f32[1792]{0:T(1024)S(1)}, f32[1792]{0:T(1024)S(1)}, f32[1792]{0:T(1024)S(1)}, /*index=5*/f32[512,1792]{1,0:T(8,128)S(1)}) fusion(f32[512,1792]{1,0:T(8,128)S(1)} %copy-done.2, f32[512,3352]{1,0:T(8,128)} %copy-done.5, f32[512,1792]{1,0:T(8,128)S(1)} %copy-done.6, ...), kind=kLoop, calls=%fused_computation.12 | loop fusion | flops 18341120 | bytes 18385920 | tf_op jit(solution)/shard_map/transpose(jvp())/reduce_sum | solution.py:238
  159.2 2.9 %pad_add_fusion = f32[512,1792]{1,0:T(8,128)} fusion(f32[512,1792]{1,0:T(8,128)S(1)} %get-tuple-element.75, f32[512,1792]{1,0:T(8,128)S(1)} %get-tuple-element.76, f32[512,1792]{1,0:T(8,128)S(1)} %get-tuple-element.77, f32[512,1792]{1,0:T(8,128)S(1)} %get-tuple-element.74), kind=kLoop, calls=%fused_computation.7 | loop fusion | flops 2752512 | bytes 18350080 | tf_op jit(solution)/shard_map/transpose(jvp())/add_any | solution.py:238
  162.3 1.7 fusion.50
  164.0 3.6 %add_convert_fusion = bf16[512,3352]{1,0:T(8,128)(2,1)S(1)} fusion(f32[512,1536]{1,0:T(8,128)} %get-tuple-element.73, f32[512,1792]{1,0:T(8,128)} %pad_add_fusion, f32[512,24]{1,0:T(8,128)S(1)} %get-tuple-element.67), kind=kLoop, calls=%fused_computation | loop fusion | flops 5148672 | bytes 10297344 | tf_op jit(solution)/shard_map/convert_element_type | solution.py:565
  168.8 3.3 %fusion.11 = (f32[768]{0:T(1024)S(1)}, f32[512]{0:T(512)S(1)}, f32[512,768]{1,0:T(8,128)S(1)}) fusion(bf16[512,768]{1,0:T(8,128)(2,1)S(1)} %copy-done.10, f32[512]{0:T(512)S(1)} %fusion.38, f32[768]{0:T(1024)S(1)} %reshape.314, bf16[512,3352]{1,0:T(8,128)(2,1)S(1)} %add_convert_fusion, bf16[768,1048]{1,0:T(8,128)(2,1)S(1)} %bitcast.104, ...), kind=kOutput, calls=%fused_computation.50 | convolution fusion | flops 2654317312 | bytes 10950656 | tf_op jit(solution)/shard_map/dot_general | solution.py:32
  172.1 1.6 fusion.12
  179.1 2.3 convolution_convert_fusion
  181.4 4.0 %copy.90 = bf16[768,1048]{1,0:T(8,128)(2,1)} copy(bf16[768,1048]{0,1:T(8,128)(2,1)} %convolution_convert_fusion) | data formatting | bytes 3219456 | tf_op jit(solution)/shard_map/convert_element_type | solution.py:576
  185.4 2.9 %copy.91 = bf16[2,2,2,2,2,24,1048]{6,5,4,3,2,1,0:T(8,128)(2,1)} copy(bf16[2,2,2,2,2,24,1048]{6,5,0,2,3,1,4:T(8,128)(2,1)} %bitcast.93) | data formatting | bytes 3219456 | tf_op jit(solution)/shard_map/transpose | solution.py:488
  188.3 1.6 convolution_convert_fusion.1
  194.0 54.2 %reduce_grads.1 = (bf16[4,24,1152]{2,1,0:T(8,128)(2,1)}, bf16[4,24,1152]{2,1,0:T(8,128)(2,1)}, bf16[4,24,1048]{2,1,0:T(8,128)(2,1)}, bf16[4,48,256]{2,1,0:T(8,12...) custom-call(bf16[32,24,1152]{2,1,0:T(8,128)(2,1)} %bitcast.94, ...), custom_call_target="tpu_custom_call" | custom-call | tf_op jit(solution)/shard_map/reduce_grads/pallas_call | solution.py:469
  249.5 2.3 maximum_convert_fusion
  257.3 1.8 maximum_convert_fusion.1
  (133 shorter events, 33.8 us)
Async XLA Ops:
  58.4 4.5 %copy-start.24 = (bf16[32,48,256]{2,1,0:T(8,128)(2,1)S(1)}, bf16[32,48,256]{2,1,0:T(8,128)(2,1)}, u32[]{:S(2)}) copy-start(bf16[32,48,256]{2,1,0:T(8,128)(2,1)} %get-tuple-element.35) | copy-start | bytes 2359300
  58.4 6.1 %copy-start.17 = (bf16[32,24,1048]{2,1,0:T(8,128)(2,1)S(1)}, bf16[32,24,1048]{2,1,0:T(8,128)(2,1)}, u32[]{:S(2)}) copy-start(bf16[32,24,1048]{2,1,0:T(8,128)(2,1)} %get-tuple-element.34) | copy-start | bytes 4829188
  60.7 4.1 %copy-start.16 = (bf16[32,24,1152]{2,1,0:T(8,128)(2,1)S(1)}, bf16[32,24,1152]{2,1,0:T(8,128)(2,1)}, u32[]{:S(2)}) copy-start(bf16[32,24,1152]{2,1,0:T(8,128)(2,1)} %get-tuple-element.33) | copy-start | bytes 5308420
  64.7 3.9 %copy-start.11 = (bf16[2,2,2,2,2,24,1048]{6,5,0,2,3,1,4:T(8,128)(2,1)}, bf16[2,2,2,2,2,24,1048]{6,5,0,2,3,1,4:T(8,128)(2,1)S(1)}, u32[]{:S(2)}) copy-start(bf16[2,2,2,2,2,24,1048]{6,5,0,2,3,1,4:T(8,128)(2,1)S(1)} %copy.78) | copy-start | bytes 4829188
  64.8 3.6 %copy-start.29 = (bf16[8,16,128]{2,1,0:T(8,128)(2,1)S(1)}, bf16[8,16,128]{2,1,0:T(8,128)(2,1)}, u32[]{:S(2)}) copy-start(bf16[8,16,128]{2,1,0:T(8,128)(2,1)} %get-tuple-element.31) | copy-start | bytes 98308
  64.8 3.6 %copy-start.9 = (bf16[512,768]{1,0:T(8,128)(2,1)S(1)}, bf16[512,768]{1,0:T(8,128)(2,1)}, u32[]{:S(2)}) copy-start(bf16[512,768]{1,0:T(8,128)(2,1)} %param.12) | copy-start | bytes 2359300
  73.8 4.1 %copy-start.5 = (f32[512,3352]{1,0:T(8,128)}, f32[512,3352]{1,0:T(8,128)S(1)}, u32[]{:S(2)}) copy-start(f32[512,3352]{1,0:T(8,128)S(1)} %fusion.7) | copy-start | bytes 20594692
  87.0 2.8 %copy-start = (f32[512,1792]{1,0:T(8,128)}, f32[512,1792]{1,0:T(8,128)S(1)}, u32[]{:S(2)}) copy-start(f32[512,1792]{1,0:T(8,128)S(1)} %get-tuple-element.71) | copy-start | bytes 11010052
  87.0 2.8 %copy-start.30 = (f32[24]{0:T(128)S(1)}, f32[24]{0:T(128)}, u32[]{:S(2)}) copy-start(f32[24]{0:T(128)} %param.19) | copy-start | bytes 292
  87.0 4.7 %copy-start.33 = (f32[24]{0:T(128)S(1)}, f32[24]{0:T(128)}, u32[]{:S(2)}) copy-start(f32[24]{0:T(128)} %param.20) | copy-start | bytes 292
  92.2 2.8 %copy-start.25 = (f32[512,24]{0,1:T(8,128)}, f32[512,24]{0,1:T(8,128)S(1)}, u32[]{:S(2)}) copy-start(f32[512,24]{0,1:T(8,128)S(1)} %fusion.22) | copy-start | bytes 147460
  95.0 12.7 %copy-start.31 = (f32[24]{0:T(128)S(1)}, f32[24]{0:T(128)}, u32[]{:S(2)}) copy-start(f32[24]{0:T(128)} %param.21) | copy-start | bytes 292
  112.7 7.1 %copy-start.7 = (f32[512,1536]{1,0:T(8,128)}, f32[512,1536]{1,0:T(8,128)S(1)}, u32[]{:S(2)}) copy-start(f32[512,1536]{1,0:T(8,128)S(1)} %get-tuple-element.70) | copy-start | bytes 9437188
  112.9 5.2 %copy-start.18 = (bf16[512,768]{1,0:T(8,128)(2,1)S(1)}, bf16[512,768]{1,0:T(8,128)(2,1)}, u32[]{:S(2)}) copy-start(bf16[512,768]{1,0:T(8,128)(2,1)} %param.13) | copy-start | bytes 2359300
  112.9 5.2 %copy-start.21 = (bf16[2,2,2,2,2,48,256]{6,5,0,2,3,1,4:T(8,128)(2,1)S(1)}, bf16[2,2,2,2,2,48,256]{6,5,0,2,3,1,4:T(8,128)(2,1)}, u32[]{:S(2)}) copy-start(bf16[2,2,2,2,2,48,256]{6,5,0,2,3,1,4:T(8,128)(2,1)} %copy.85) | copy-start | bytes 2359300
  112.9 5.2 %copy-start.22 = (bf16[2,2,2,2,2,48,256]{6,5,0,3,1,2,4:T(8,128)(2,1)S(1)}, bf16[2,2,2,2,2,48,256]{6,5,0,3,1,2,4:T(8,128)(2,1)}, u32[]{:S(2)}) copy-start(bf16[2,2,2,2,2,48,256]{6,5,0,3,1,2,4:T(8,128)(2,1)} %copy.84) | copy-start | bytes 2359300
  112.9 5.2 %copy-start.23 = (bf16[2,2,2,2,2,48,256]{6,5,0,1,2,3,4:T(8,128)(2,1)S(1)}, bf16[2,2,2,2,2,48,256]{6,5,0,1,2,3,4:T(8,128)(2,1)}, u32[]{:S(2)}) copy-start(bf16[2,2,2,2,2,48,256]{6,5,0,1,2,3,4:T(8,128)(2,1)} %copy.83) | copy-start | bytes 2359300
  118.1 3.0 %copy-start.3 = (f32[512,1536]{1,0:T(8,128)S(1)}, f32[512,1536]{1,0:T(8,128)}, u32[]{:S(2)}) copy-start(f32[512,1536]{1,0:T(8,128)} %jvp_scan_fwd_.1) | copy-start | bytes 9437188
  126.9 22.0 %copy-start.4 = (f32[512,1536]{1,0:T(8,128)S(1)}, f32[512,1536]{1,0:T(8,128)}, u32[]{:S(2)}) copy-start(f32[512,1536]{1,0:T(8,128)} %get-tuple-element.65.dy_ref) | copy-start | bytes 9437188
  149.0 3.0 %copy-start.2 = (f32[512,1792]{1,0:T(8,128)S(1)}, f32[512,1792]{1,0:T(8,128)}, u32[]{:S(2)}) copy-start(f32[512,1792]{1,0:T(8,128)} %slice.178) | copy-start | bytes 11010052
  149.0 4.1 %copy-start.6 = (f32[512,1792]{1,0:T(8,128)S(1)}, f32[512,1792]{1,0:T(8,128)}, u32[]{:S(2)}) copy-start(f32[512,1792]{1,0:T(8,128)} %get-tuple-element.72) | copy-start | bytes 11010052
  149.0 4.1 %copy-start.26 = (f32[512,128]{1,0:T(8,128)S(1)}, f32[512,128]{1,0:T(8,128)}, u32[]{:S(2)}) copy-start(f32[512,128]{1,0:T(8,128)} %get-tuple-element.42) | copy-start | bytes 786436
  149.0 4.1 %copy-start.27 = (f32[512,128]{1,0:T(8,128)S(1)}, f32[512,128]{1,0:T(8,128)}, u32[]{:S(2)}) copy-start(f32[512,128]{1,0:T(8,128)} %get-tuple-element.41) | copy-start | bytes 786436
  159.2 3.0 %copy-start.28 = (f32[512,128]{1,0:T(8,128)S(1)}, f32[512,128]{1,0:T(8,128)}, u32[]{:S(2)}) copy-start(f32[512,128]{1,0:T(8,128)} %get-tuple-element.39) | copy-start | bytes 786436
  159.2 3.1 %copy-start.32 = (f32[24,512]{1,0:T(8,128)S(1)}, f32[24,512]{1,0:T(8,128)}, u32[]{:S(2)}) copy-start(f32[24,512]{1,0:T(8,128)} %get-tuple-element.40) | copy-start | bytes 147460
  164.0 3.6 %copy-start.10 = (bf16[512,768]{1,0:T(8,128)(2,1)S(1)}, bf16[512,768]{1,0:T(8,128)(2,1)}, u32[]{:S(2)}) copy-start(bf16[512,768]{1,0:T(8,128)(2,1)} %param.12) | copy-start | bytes 2359300
  164.0 3.7 %copy-start.12 = (bf16[2,2,2,2,2,24,1048]{6,5,0,2,3,1,4:T(8,128)(2,1)S(1)}, bf16[2,2,2,2,2,24,1048]{6,5,0,2,3,1,4:T(8,128)(2,1)}, u32[]{:S(2)}) copy-start(bf16[2,2,2,2,2,24,1048]{6,5,0,2,3,1,4:T(8,128)(2,1)} %copy-done.11) | copy-start | bytes 4829188
  164.0 4.3 %copy-start.13 = (bf16[2,2,2,2,2,24,1152]{6,5,0,3,1,2,4:T(8,128)(2,1)S(1)}, bf16[2,2,2,2,2,24,1152]{6,5,0,3,1,2,4:T(8,128)(2,1)}, u32[]{:S(2)}) copy-start(bf16[2,2,2,2,2,24,1152]{6,5,0,3,1,2,4:T(8,128)(2,1)} %copy.77) | copy-start | bytes 5308420
  164.0 4.8 %copy-start.14 = (bf16[2,2,2,2,2,24,1152]{6,5,0,1,2,3,4:T(8,128)(2,1)S(1)}, bf16[2,2,2,2,2,24,1152]{6,5,0,1,2,3,4:T(8,128)(2,1)}, u32[]{:S(2)}) copy-start(bf16[2,2,2,2,2,24,1152]{6,5,0,1,2,3,4:T(8,128)(2,1)} %copy.76) | copy-start | bytes 5308420
  168.8 3.3 %copy-start.19 = (bf16[512,768]{1,0:T(8,128)(2,1)S(1)}, bf16[512,768]{1,0:T(8,128)(2,1)}, u32[]{:S(2)}) copy-start(bf16[512,768]{1,0:T(8,128)(2,1)} %param.13) | copy-start | bytes 2359300
  181.4 6.9 %copy-start.8 = (f32[512,1536]{1,0:T(8,128)S(1)}, f32[512,1536]{1,0:T(8,128)}, u32[]{:S(2)}) copy-start(f32[512,1536]{1,0:T(8,128)} %copy-done.7) | copy-start | bytes 9437188
  185.4 2.9 %copy-start.20 = (bf16[512,768]{1,0:T(8,128)(2,1)S(1)}, bf16[512,768]{1,0:T(8,128)(2,1)}, u32[]{:S(2)}) copy-start(bf16[512,768]{1,0:T(8,128)(2,1)} %param.13) | copy-start | bytes 2359300
  (2 other events, 4.4 us)
where the time goes:
time: 260 us; the launch traced here: 259 us
  Pallas kernels  139 us (53%)
  local copies, waits for them, and re-layouts  52.5 us (20%)
  other arithmetic  41.9 us (16%)
  matrix products  24 us (9%)
    pallas_call x1, Pallas kernels, reduce_all(): pl.pallas_call(functools.partial(reduce_kernel, plan, bits_of('rep')), in...  54.2 us
    pallas_call x1, Pallas kernels, gather_all(): pl.pallas_call(functools.partial(gather_kernel, plan), in_specs=[vmem] *...  50 us
    pallas_call x1, Pallas kernels, mixer_core(): mixed = span_scan(values, step, cum, keys_b, query_c)  22 us
    pallas_call x1, Pallas kernels, span_scan(): pl.pallas_call(scan_fwd_kernel, grid=(NH // PAIR,), in_specs=scan_specs(l...  12.7 us
    dot_general x6, matrix products, contract(): lax.dot_general(left, right, (((left_dim,), (right_dim,)), ((), ())), pre...  11.5 us
    mul x1, other arithmetic, mixer_core(): active = jax.nn.silu(conv_out)  8.37 us
    reshape x6, local copies, waits for them, and re-layouts, from_order(): split = blocks.reshape((2,) * len(labels) + blocks.shape[1:])  8.32 us
    unnamed x69, local copies, waits for them, and re-layouts  6.99 us

commit v1 on v0

--- a/solution.py
+++ b/solution.py
@@ -61,7 +61,7 @@
     return lax.broadcasted_iota(jnp.int32, shape, 1) // HD
 
 
-def scan_fwd_kernel(x_ref, dt_ref, cum_ref, cumt_ref, b_ref, c_ref, y_ref, score):
+def scan_fwd_kernel(x_ref, dt_ref, cum_ref, cumt_ref, b_ref, c_ref, skip_ref, y_ref, score):
     pair = pl.program_id(0)
     length = x_ref.shape[0]
     half, tiles = tiles_of(length)
@@ -86,12 +86,13 @@
             term = contract(mixed, scaled[col * half : (col + 1) * half], 1, 0)
             sums[row] = term if sums[row] is None else sums[row] + term
     for row in range(2):
-        y_ref[row * half : (row + 1) * half, :] = sums[row]
+        rows = slice(row * half, (row + 1) * half)
+        y_ref[rows, :] = sums[row] + skip_ref[...] * x[rows]
 
 
 def scan_bwd_kernel(
-    x_ref, dt_ref, cum_ref, cumt_ref, b_ref, c_ref, dy_ref,
-    dx_ref, ddt_ref, drow_ref, dcol_ref, db_ref, dc_ref, score, dscore,
+    x_ref, dt_ref, cum_ref, cumt_ref, b_ref, c_ref, skip_ref, dy_ref,
+    dx_ref, ddt_ref, drow_ref, dcol_ref, db_ref, dc_ref, dskip_ref, score, dscore,
 ):
     pair = pl.program_id(0)
     length = x_ref.shape[0]
@@ -108,6 +109,7 @@
     lane = lax.broadcasted_iota(jnp.int32, x_ref.shape, 1)
     x = x_ref[...]
     dy = dy_ref[...]
+    dskip_ref[...] = jnp.sum(x * dy, axis=0, keepdims=True)
     d_scaled = [None, None]
     dt_pair = jnp.zeros_like(x)
     for sub in range(PAIR):
@@ -141,7 +143,7 @@
             dcol_ref[pl.ds(head, 1), span] = col_sum[part_index]
     for part_index in range(2):
         span = slice(part_index * half, (part_index + 1) * half)
-        dx_ref[span, :] = d_scaled[part_index] * dt_pair[span]
+        dx_ref[span, :] = d_scaled[part_index] * dt_pair[span] + skip_ref[...] * dy[span]
         products = d_scaled[part_index] * x[span]
         for sub in range(PAIR):
             head = pair * PAIR + sub
@@ -160,9 +162,9 @@
     return pl.BlockSpec(shape, lambda pair: (0, 0))
 
 
-def scan_operands(x, dt, cum):
+def scan_operands(active, dt, cum, skip):
     pad = ((0, 0), (0, LANES - NH))
-    return x, jnp.pad(dt, pad), jnp.pad(cum, pad), cum.T
+    return active, jnp.pad(dt, pad), jnp.pad(cum, pad), cum.T, active, active, skip
 
 
 def scan_specs(length):
@@ -172,56 +174,60 @@
         lanes,
         lanes,
         whole_spec((NH, length)),
-        whole_spec((length, NS)),
-        whole_spec((length, NS)),
+        pl.BlockSpec((length, NS), lambda pair: (0, DI // NS)),
+        pl.BlockSpec((length, NS), lambda pair: (0, DI // NS + 1)),
+        pl.BlockSpec((1, LANES), lambda pair: (0, pair)),
     ]
 
 
 @jax.custom_vjp
-def span_scan(x, dt, cum, keys_b, query_c):
-    length = x.shape[0]
+def span_scan(active, dt, cum, skip):
+    length = active.shape[0]
     return pl.pallas_call(
         scan_fwd_kernel,
         grid=(NH // PAIR,),
         in_specs=scan_specs(length),
         out_specs=pl.BlockSpec((length, LANES), lambda pair: (0, pair)),
-        out_shape=jax.ShapeDtypeStruct(x.shape, jnp.float32),
+        out_shape=jax.ShapeDtypeStruct((length, DI), jnp.float32),
         scratch_shapes=[pltpu.VMEM((length, length), jnp.float32)],
         name="scan_fwd",
-    )(*scan_operands(x, dt, cum), keys_b, query_c)
-
-
-def span_scan_fwd(x, dt, cum, keys_b, query_c):
-    return span_scan(x, dt, cum, keys_b, query_c), (x, dt, cum, keys_b, query_c)
+    )(*scan_operands(active, dt, cum, skip))
+
+
+def span_scan_fwd(active, dt, cum, skip):
+    return span_scan(active, dt, cum, skip), (active, dt, cum, skip)
 
 
 def span_scan_bwd(saved, dy):
-    x, dt, cum, keys_b, query_c = saved
-    length = x.shape[0]
+    active, dt, cum, skip = saved
+    length = active.shape[0]
     pair_block = pl.BlockSpec((length, LANES), lambda pair: (0, pair))
     lanes = whole_spec((length, LANES))
     square = pltpu.VMEM((length, length), jnp.float32)
     f32 = jnp.float32
-    dx, ddt, drow, dcol, db, dc = pl.pallas_call(
+    dx, ddt, drow, dcol, db, dc, dskip = pl.pallas_call(
         scan_bwd_kernel,
         grid=(NH // PAIR,),
         in_specs=scan_specs(length) + [pair_block],
         out_specs=[
             pair_block, lanes, lanes, whole_spec((NH, length)),
             whole_spec((length, NS)), whole_spec((length, NS)),
+            pl.BlockSpec((1, LANES), lambda pair: (0, pair)),
         ],
         out_shape=[
-            jax.ShapeDtypeStruct(x.shape, f32),
+            jax.ShapeDtypeStruct((length, DI), f32),
             jax.ShapeDtypeStruct((length, LANES), f32),
             jax.ShapeDtypeStruct((length, LANES), f32),
             jax.ShapeDtypeStruct((NH, length), f32),
             jax.ShapeDtypeStruct((length, NS), f32),
             jax.ShapeDtypeStruct((length, NS), f32),
+            jax.ShapeDtypeStruct((1, DI), f32),
         ],
         scratch_shapes=[square, square],
         name="scan_bwd",
-    )(*scan_operands(x, dt, cum), keys_b, query_c, dy)
-    return dx, ddt[:, :NH], drow[:, :NH] - dcol.T, db, dc
+    )(*scan_operands(active, dt, cum, skip), dy)
+    d_active = jnp.concatenate([dx, db, dc], axis=1)
+    return d_active, ddt[:, :NH], drow[:, :NH] - dcol.T, dskip
 
 
 span_scan.defvjp(span_scan_fwd, span_scan_bwd)
@@ -237,15 +243,11 @@
     for offset in range(KCONV):
         conv_out = conv_out + conv_w[offset] * padded[offset : offset + length]
     active = jax.nn.silu(conv_out)
-    values = active[:, :DI]
-    keys_b = active[:, DI : DI + NS]
-    query_c = active[:, DI + NS :]
     step = jax.nn.softplus(step_raw + step_bias)
     logdecay = -step * jnp.exp(decay_log)
     causal = (jnp.arange(length)[:, None] >= jnp.arange(length)[None, :]).astype(jnp.float32)
     cum = jnp.dot(causal, logdecay, precision=HIGH)
-    mixed = span_scan(values, step, cum, keys_b, query_c)
-    mixed = mixed + jnp.repeat(skip_weight, HD) * values
+    mixed = span_scan(active, step, cum, jnp.repeat(skip_weight, HD)[None])
     flat = mixed * jax.nn.silu(gate)
     scale = lax.rsqrt(jnp.mean(flat * flat, axis=-1, keepdims=True) + EPS)
     return flat * scale * mix_gain
@@ -495,6 +497,10 @@
     return split.transpose(perm).reshape((-1, blocks.shape[-1]))
 
 
+def whole_lanes(array):
+    return jnp.pad(array, ((0, 0), (0, -array.shape[1] % LANES)))
+
+
 def my_rows(shard):
     count = shard.shape[0] // lax.axis_size("rep")
     return lax.dynamic_slice_in_dim(shard, lax.axis_index("rep") * count, count, 0)
@@ -570,14 +576,14 @@
     vectors = [d_gain, d_cw.reshape(-1), d_cb, d_mg, d_sb, d_dl, d_sk]
     packed = jnp.concatenate(vectors)
     packed = jnp.pad(packed, (0, -packed.size % 1024)).reshape(-1, LANES)
-    partial = [contract(normed_b, d_proj_b[:, cut], 0, 0) for cut in columns]
+    partial = [contract(normed_b, whole_lanes(d_proj_b[:, cut]), 0, 0) for cut in columns]
     partial += [d_out_w[:, cut] for cut in out_columns]
     blocks = [
         to_order(part.astype(jnp.bfloat16), order) for part, order in zip(partial, wide_plan)
     ]
     *sums, packed = reduce_all(wide_plan, blocks, packed)
     sums = [part.reshape(-1, part.shape[-1]) for part in sums]
-    g_in = jnp.concatenate(sums[: len(columns)], axis=1).astype(jnp.float32)
+    g_in = jnp.concatenate(sums[: len(columns)], axis=1)[:, :PROJ].astype(jnp.float32)
     g_out = jnp.concatenate(sums[len(columns) :], axis=1).astype(jnp.float32)
     packed = packed.reshape(-1)
     totals = []

time: 260 us -> 253 us (0.973)
  other arithmetic: 41.9 us -> 36.3 us
    mul x0 -> x1, other arithmetic: none -> 5.45 us  [mixer_core(): flat = mixed * jax.nn.silu(gate)]
    reduce_sum x2 -> x1, other arithmetic: 5.96 us -> 0.63 us  [mixer_core(): mixed = span_scan(active, step, cum, jnp.repeat(skip_weight, HD)[None])]
    slice x2, local copies, waits for them, and re-layouts: 4.29 us -> 0.01 us  [body(): d_proj_b[:, cut]]
    mul x1, other arithmetic: 8.37 us -> 4.23 us  [mixer_core(): active = jax.nn.silu(conv_out)]
    convert_element_type x1 -> x0, local copies, waits for them, and re-layouts: 3.96 us -> none  [body(): part.astype(jnp.bfloat16)]
    unnamed x69 -> x101, local copies, waits for them, and re-layouts: 6.99 us -> 10.5 us
    transpose x1 -> x0, local copies, waits for them, and re-layouts: 2.92 us -> none  [to_order(): return split.transpose(perm).reshape((-1, rows, array.shape[1]))]
    dot_general x1, matrix products: 5.16 us -> 2.35 us  [body(): branch = jnp.dot(gated_b, out_full, preferred_element_type=jnp.float32)]
where the time goes in v1:
time: 253 us; the launch traced here: 252 us
  Pallas kernels  139 us (55%)
  local copies, waits for them, and re-layouts  53.1 us (21%)
  other arithmetic  36.3 us (14%)
  matrix products  21.6 us (9%)
    pallas_call x1, Pallas kernels, reduce_all(): pl.pallas_call(functools.partial(reduce_kernel, plan, bits_of('rep')), in...  54.3 us
    pallas_call x1, Pallas kernels, gather_all(): pl.pallas_call(functools.partial(gather_kernel, plan), in_specs=[vmem] *...  50 us
    pallas_call x1, Pallas kernels, mixer_core(): mixed = span_scan(active, step, cum, jnp.repeat(skip_weight, HD)[None])  22.3 us
    pallas_call x1, Pallas kernels, span_scan(): pl.pallas_call(scan_fwd_kernel, grid=(NH // PAIR,), in_specs=scan_specs(l...  12.7 us
    dot_general x6, matrix products, contract(): lax.dot_general(left, right, (((left_dim,), (right_dim,)), ((), ())), pre...  12.6 us
    unnamed x101, local copies, waits for them, and re-layouts  10.5 us
    reshape x6, local copies, waits for them, and re-layouts, from_order(): split = blocks.reshape((2,) * len(labels) + blocks.shape[1:])  7.54 us
    reshape x6, local copies, waits for them, and re-layouts, to_order(): split = array.reshape((2,) * len(labels) + (rows, array.shape[1]))  7 us

profile of v1, /device:TPU:0, one launch (start us, length us, event | category | flops | bytes accessed | tf_op | source)
XLA Modules:
  0.0 252.2 jit_solution(6823790517469977771)
XLA Ops:
  5.2 2.1 concatenate.21
  9.8 1.4 dynamic-slice_bitcast_fusion.refs_3_
  11.3 1.4 dynamic-slice_bitcast_fusion.3
  12.7 1.5 dynamic-slice_bitcast_fusion.1
  14.2 50.0 %gather_weights.1 = (bf16[8,16,128]{2,1,0:T(8,128)(2,1)}, bf16[32,24,1152]{2,1,0:T(8,128)(2,1)}, bf16[32,24,1152]{2,1,0:T(8,128)(2,1)}, bf16[32,24,1048]{2,1,0:T...) custom-call(bf16[1,16,128]{2,1,0:T(8,128)(2,1)} %pad_bitcast_fusion.1.refs_0_, ...), custom_call_target="tpu_custom_call" | custom-call | tf_op jit(solution)/shard_map/gather_weights/pallas_call | solution.py:355
  65.1 1.7 copy.55
  69.7 2.1 copy.62
  73.7 1.7 copy.56
  75.7 3.1 %fusion.7 = f32[512,3352]{1,0:T(8,128)S(1)} fusion(bf16[768,1048]{1,0:T(8,128)(2,1)S(1)} %bitcast.106, bf16[768,1152]{1,0:T(8,128)(2,1)S(1)} %bitcast.104, bf16[768,1152]{1,0:T(8,128)(2,1)S(1)} %bitcast.102, bf16[512,768]{1,0:T(8,128)(2,1)S(1)} %copy-done.7, f32[768]{0:T(1024)S(1)} %reshape.314, f32[512]{0:T(512)S(1)} %fusion.39), kind=kOutput, calls=%fused_computation.39 | convolution fusion | flops 2653138944 | bytes 12805120 | tf_op jit(solution)/shard_map/dot_general | solution.py:550
  78.8 2.9 %copy-done.3 = f32[512,3352]{1,0:T(8,128)} copy-done((f32[512,3352]{1,0:T(8,128)}, f32[512,3352]{1,0:T(8,128)S(1)}, u32[]{:S(2)}) %copy-start.3) | copy-done | bytes 6864920
  84.0 2.3 slice.170
  86.3 1.9 copy-done
  88.2 4.2 %fusion.2 = (f32[512,1792]{1,0:T(8,128)}, f32[512,1792]{1,0:T(8,128)}) fusion(f32[512,1792]{1,0:T(8,128)S(1)} %slice.170, f32[1792]{0:T(1024)S(1)} %mul.304, f32[1792]{0:T(1024)S(1)} %mul.301, f32[1792]{0:T(1024)S(1)} %copy-done.28, f32[1792]{0:T(1024)S(1)} %mul.290, f32[1792]{0:T(1024)S(1)} %copy-done.31), kind=kLoop, calls=%fused_computation.15 | loop fusion | flops 11010048 | bytes 11045888 | tf_op jit(solution)/shard_map/jvp(jit(silu))/mul | solution.py:245
  92.4 12.7 %jvp_scan_fwd_.1 = f32[512,1536]{1,0:T(8,128)} custom-call(f32[512,1792]{1,0:T(8,128)} %get-tuple-element.71.x_ref.b_ref.c_ref, f32[512,128]{1,0:T(8,128)} %pad.65.dt_ref, f32[512,128]{1,0:T(8,128)} %pad.66.cum_ref, f32[24,512]{1,0:T(8,128)} %bitcast.123, f32[512,1792]{1,0:T(8,128)} %get-tuple-element.71.x_ref.b_ref.c_ref, ...), custom_call_target="tpu_custom_call" | custom-call | tf_op jit(solution)/shard_map/jvp(scan_fwd)/pallas_call | solution.py:186
  105.2 4.0 %multiply_reduce_fusion.6 = (f32[512]{0:T(512)S(1)}, f32[512,1536]{1,0:T(8,128)S(1)}) fusion(f32[512,1536]{1,0:T(8,128)} %jvp_scan_fwd_.1, f32[512,3352]{1,0:T(8,128)} %copy-done.3), kind=kLoop, calls=%fused_computation.28 | loop fusion | flops 5504512 | bytes 9439232 | tf_op jit(solution)/shard_map/jvp()/reduce_sum | solution.py:252
  109.2 2.3 fusion.14
  111.6 2.3 multiply_reduce_fusion.4
  113.9 5.5 %fusion.16 = (f32[512,1536]{1,0:T(8,128)}, f32[512,1536]{1,0:T(8,128)}) fusion(f32[512,1536]{1,0:T(8,128)S(1)} %get-tuple-element.70, f32[512]{0:T(512)S(1)} %multiply_multiply_fusion.1, f32[512,1536]{1,0:T(8,128)S(1)} %get-tuple-element.91, f32[1536]{0:T(1024)S(1)} %copy-done.30, f32[512]{0:T(512)S(1)} %fusion.40, f32[512,3352]{1,0:T(8,128)} %copy-done.3, ...), kind=kLoop, calls=%fused_computation.52 | loop fusion | flops 13369344 | bytes 18884608 | tf_op jit(solution)/shard_map/transpose(jvp())/mul | solution.py:251
  119.4 3.0 %convolution_convert_fusion = bf16[1536,768]{1,0:T(8,128)(2,1)} fusion(bf16[512,768]{1,0:T(8,128)(2,1)S(1)} %copy-done.16, bf16[512]{0:T(512)(128)(2,1)S(1)} %copy-done.42, f32[512,1536]{1,0:T(8,128)S(1)} %get-tuple-element.70, f32[1536]{0:T(1024)S(1)} %copy-done.30, f32[512]{0:T(512)S(1)} %fusion.40), kind=kOutput, calls=%fused_computation.19 | convolution fusion | flops 1211891712 | bytes 6300672 | tf_op jit(solution)/shard_map/dot_general | solution.py:32
  122.4 22.3 %transpose_jvp_scan_bwd__.1 = (f32[512,1536]{1,0:T(8,128)}, f32[512,128]{1,0:T(8,128)}, f32[512,128]{1,0:T(8,128)}, f32[24,512]{1,0:T(8,128)}, f32[512,128]{1,0:...) custom-call(f32[512,1792]{1,0:T(8,128)} %get-tuple-element.71.x_ref.b_ref.c_ref, f32[512,128]{1,0:T(8,128)} %pad.65.dt_ref, ...), custom_call_target="tpu_custom_call" | custom-call | tf_op jit(solution)/shard_map/transpose(jvp(scan_bwd))/pallas_call | solution.py:250
  144.7 1.8 fusion.55
  150.4 3.0 %fusion.51 = (f32[24]{0:T(128)}, f32[512,24]{1,0:T(8,128)}, f32[24]{0:T(128)S(1)}) fusion(f32[512,24]{1,0:T(8,128)S(1)} %compare_select_fusion.2, f32[24]{0:T(128)S(1)} %copy-done.43, f32[512,3352]{1,0:T(8,128)} %copy-done.3, f32[24]{0:T(128)S(1)} %copy-done.48, f32[512,128]{1,0:T(8,128)} %get-tuple-element.39, f32[512,128]{0,1:T(8,128)S(1)} %copy.65, ...), kind=kOutput, calls=%fused_computation.123 | convolution fusion | flops 76206032 | bytes 509120 | tf_op jit(solution)/shard_map/transpose(jvp())/dot_general | solution.py:249
  155.2 1.7 copy-done.4
  158.1 6.5 %multiply_reduce_fusion.2 = (f32[1792]{0:T(1024)S(1)}, f32[1792]{0:T(1024)S(1)}, f32[1792]{0:T(1024)S(1)}, f32[1792]{0:T(1024)}, f32[1792]{0:T(1024)S(1)}, /*index=5*/f32[512,1792]{1,0:T(8,128)}) fusion(f32[512,1792]{1,0:T(8,128)S(1)} %copy-done.1, f32[512,3352]{1,0:T(8,128)} %copy-done.3, f32[512,1792]{1,0:T(8,128)S(1)} %copy-done.4, ...), kind=kLoop, calls=%fused_computation.12 | loop fusion | flops 16506112 | bytes 18385920 | tf_op jit(solution)/shard_map/transpose(jvp())/reduce_sum | solution.py:244
  165.3 3.2 %broadcast_multiply_fusion = (f32[512,1792]{1,0:T(8,128)S(1)}, f32[512,1792]{1,0:T(8,128)S(1)}, f32[512,1792]{1,0:T(8,128)S(1)}, f32[512,1792]{1,0:T(8,128)S(1)}) fusion(f32[512,1792]{1,0:T(8,128)} %get-tuple-element.68, f32[1792]{0:T(1024)S(1)} %mul.304, f32[1792]{0:T(1024)S(1)} %mul.290, f32[1792]{0:T(1024)S(1)} %copy-done.28, f32[1792]{0:T(1024)S(1)} %mul.301), kind=kLoop, calls=%fused_computation.42 | loop fusion | flops 3670016 | bytes 18378752 | tf_op jit(solution)/shard_map/transpose(jvp())/mul | solution.py:244
  169.7 2.5 add_convert_fusion
  173.2 3.3 %fusion.11 = (f32[768]{0:T(1024)S(1)}, f32[512]{0:T(512)S(1)}, f32[512,768]{1,0:T(8,128)S(1)}) fusion(bf16[512,768]{1,0:T(8,128)(2,1)S(1)} %copy-done.7, f32[512]{0:T(512)S(1)} %copy-done.37, f32[768]{0:T(1024)S(1)} %copy-done.35, bf16[512,3352]{1,0:T(8,128)(2,1)S(1)} %add_convert_fusion, bf16[768,1048]{1,0:T(8,128)(2,1)S(1)} %bitcast.107, ...), kind=kOutput, calls=%fused_computation.47 | convolution fusion | flops 2654317312 | bytes 10950656 | tf_op jit(solution)/shard_map/dot_general | solution.py:32
  177.3 1.6 fusion.12
  187.0 54.3 %reduce_grads.1 = (bf16[4,24,1152]{2,1,0:T(8,128)(2,1)}, bf16[4,24,1152]{2,1,0:T(8,128)(2,1)}, bf16[4,24,1152]{2,1,0:T(8,128)(2,1)}, bf16[4,48,256]{2,1,0:T(8,12...) custom-call(bf16[32,24,1152]{2,1,0:T(8,128)(2,1)} %bitcast.94, ...), custom_call_target="tpu_custom_call" | custom-call | tf_op jit(solution)/shard_map/reduce_grads/pallas_call | solution.py:471
  241.3 1.4 fusion.56
  248.1 1.8 maximum_convert_fusion
  249.9 2.3 fusion.25
  (165 shorter events, 38.2 us)
Async XLA Ops:
  4.4 71.2 %copy-start.36 = (f32[512]{0:T(512)}, f32[512]{0:T(512)S(1)}, u32[]{:S(2)}) copy-start(f32[512]{0:T(512)S(1)} %fusion.39) | copy-start | bytes 6148
  64.2 7.6 %copy-start.19 = (bf16[32,48,256]{2,1,0:T(8,128)(2,1)S(1)}, bf16[32,48,256]{2,1,0:T(8,128)(2,1)}, u32[]{:S(2)}) copy-start(bf16[32,48,256]{2,1,0:T(8,128)(2,1)} %get-tuple-element.37) | copy-start | bytes 2359300
  65.0 7.7 %copy-start.18 = (bf16[32,48,256]{2,1,0:T(8,128)(2,1)S(1)}, bf16[32,48,256]{2,1,0:T(8,128)(2,1)}, u32[]{:S(2)}) copy-start(bf16[32,48,256]{2,1,0:T(8,128)(2,1)} %get-tuple-element.38) | copy-start | bytes 2359300
  66.7 8.9 %copy-start.9 = (bf16[2,2,2,2,2,24,1152]{6,5,0,1,2,3,4:T(8,128)(2,1)}, bf16[2,2,2,2,2,24,1152]{6,5,0,1,2,3,4:T(8,128)(2,1)S(1)}, u32[]{:S(2)}) copy-start(bf16[2,2,2,2,2,24,1152]{6,5,0,1,2,3,4:T(8,128)(2,1)S(1)} %copy.55) | copy-start | bytes 5308420
  66.8 8.8 %copy-start.34 = (f32[768]{0:T(1024)}, f32[768]{0:T(1024)S(1)}, u32[]{:S(2)}) copy-start(f32[768]{0:T(1024)S(1)} %reshape.314) | copy-start | bytes 9220
  71.8 3.6 %copy-start.15 = (bf16[32,24,1048]{2,1,0:T(8,128)(2,1)S(1)}, bf16[32,24,1048]{2,1,0:T(8,128)(2,1)}, u32[]{:S(2)}) copy-start(bf16[32,24,1048]{2,1,0:T(8,128)(2,1)} %get-tuple-element.35) | copy-start | bytes 4829188
  75.6 6.1 %copy-start.43 = (f32[24]{0:T(128)S(1)}, f32[24]{0:T(128)}, u32[]{:S(2)}) copy-start(f32[24]{0:T(128)} %param.19) | copy-start | bytes 292
  75.6 6.2 %copy-start.48 = (f32[24]{0:T(128)S(1)}, f32[24]{0:T(128)}, u32[]{:S(2)}) copy-start(f32[24]{0:T(128)} %exp.21) | copy-start | bytes 292
  82.4 3.9 %copy-start.23 = (f32[512,24]{0,1:T(8,128)}, f32[512,24]{0,1:T(8,128)S(1)}, u32[]{:S(2)}) copy-start(f32[512,24]{0,1:T(8,128)S(1)} %fusion.21) | copy-start | bytes 147460
  84.0 4.2 %copy-start.28 = (f32[1792]{0:T(1024)S(1)}, f32[1792]{0:T(1024)}, u32[]{:S(2)}) copy-start(f32[1792]{0:T(1024)} %mul.298) | copy-start | bytes 21508
  84.0 4.2 %copy-start.31 = (f32[1792]{0:T(1024)S(1)}, f32[1792]{0:T(1024)}, u32[]{:S(2)}) copy-start(f32[1792]{0:T(1024)} %reshape.313) | copy-start | bytes 21508
  105.1 4.0 %copy-start.20 = (bf16[2,2,2,2,2,48,256]{6,5,0,1,2,3,4:T(8,128)(2,1)S(1)}, bf16[2,2,2,2,2,48,256]{6,5,0,1,2,3,4:T(8,128)(2,1)}, u32[]{:S(2)}) copy-start(bf16[2,2,2,2,2,48,256]{6,5,0,1,2,3,4:T(8,128)(2,1)} %copy.62) | copy-start | bytes 2359300
  105.1 4.0 %copy-start.21 = (bf16[2,2,2,2,2,48,256]{6,5,0,3,1,2,4:T(8,128)(2,1)S(1)}, bf16[2,2,2,2,2,48,256]{6,5,0,3,1,2,4:T(8,128)(2,1)}, u32[]{:S(2)}) copy-start(bf16[2,2,2,2,2,48,256]{6,5,0,3,1,2,4:T(8,128)(2,1)} %copy.63) | copy-start | bytes 2359300
  105.1 4.0 %copy-start.22 = (bf16[2,2,2,2,2,48,256]{6,5,0,2,3,1,4:T(8,128)(2,1)S(1)}, bf16[2,2,2,2,2,48,256]{6,5,0,2,3,1,4:T(8,128)(2,1)}, u32[]{:S(2)}) copy-start(bf16[2,2,2,2,2,48,256]{6,5,0,2,3,1,4:T(8,128)(2,1)} %copy.64) | copy-start | bytes 2359300
  105.1 4.0 %copy-start.30 = (f32[1536]{0:T(1024)S(1)}, f32[1536]{0:T(1024)}, u32[]{:S(2)}) copy-start(f32[1536]{0:T(1024)} %reshape.315) | copy-start | bytes 18436
  105.2 4.0 %copy-start.41 = (f32[512]{0:T(512)S(1)}, f32[512]{0:T(512)}, u32[]{:S(2)}) copy-start(f32[512]{0:T(512)} %get-tuple-element.93) | copy-start | bytes 6148
  144.7 3.8 %copy-start.39 = (f32[1,1536]{1,0:T(1,128)S(1)}, f32[1,1536]{1,0:T(1,128)}, u32[]{:S(2)}) copy-start(f32[1,1536]{1,0:T(1,128)} %get-tuple-element.45) | copy-start | bytes 18436
  144.7 5.7 %copy-start.46 = (f32[24,512]{1,0:T(8,128)S(1)}, f32[24,512]{1,0:T(8,128)}, u32[]{:S(2)}) copy-start(f32[24,512]{1,0:T(8,128)} %get-tuple-element.41) | copy-start | bytes 147460
  146.5 6.9 %copy-start.47 = (f32[24]{0:T(128)S(1)}, f32[24]{0:T(128)}, u32[]{:S(2)}) copy-start(f32[24]{0:T(128)} %param.20) | copy-start | bytes 292
  149.2 5.9 %copy-start.25 = (f32[512,128]{1,0:T(8,128)S(1)}, f32[512,128]{1,0:T(8,128)}, u32[]{:S(2)}) copy-start(f32[512,128]{1,0:T(8,128)} %get-tuple-element.43) | copy-start | bytes 786436
  149.2 5.9 %copy-start.24 = (f32[512,128]{1,0:T(8,128)S(1)}, f32[512,128]{1,0:T(8,128)}, u32[]{:S(2)}) copy-start(f32[512,128]{1,0:T(8,128)} %get-tuple-element.44) | copy-start | bytes 786436
  150.4 4.5 %copy-start.8 = (f32[512,1536]{1,0:T(8,128)S(1)}, f32[512,1536]{1,0:T(8,128)}, u32[]{:S(2)}) copy-start(f32[512,1536]{1,0:T(8,128)} %get-tuple-element.42) | copy-start | bytes 9437188
  169.6 3.5 %copy-start.14 = (bf16[2,2,2,2,2,24,1048]{6,5,0,2,3,1,4:T(8,128)(2,1)S(1)}, bf16[2,2,2,2,2,24,1048]{6,5,0,2,3,1,4:T(8,128)(2,1)}, u32[]{:S(2)}) copy-start(bf16[2,2,2,2,2,24,1048]{6,5,0,2,3,1,4:T(8,128)(2,1)} %copy-done.13) | copy-start | bytes 4829188
  169.7 3.5 %copy-start.35 = (f32[768]{0:T(1024)S(1)}, f32[768]{0:T(1024)}, u32[]{:S(2)}) copy-start(f32[768]{0:T(1024)} %copy-done.34) | copy-start | bytes 9220
  169.7 3.5 %copy-start.37 = (f32[512]{0:T(512)S(1)}, f32[512]{0:T(512)}, u32[]{:S(2)}) copy-start(f32[512]{0:T(512)} %copy-done.36) | copy-start | bytes 6148
  173.1 3.4 %copy-start.27 = (f32[7168]{0:T(1024)S(1)}, f32[7168]{0:T(1024)}, u32[]{:S(2)}) copy-start(f32[7168]{0:T(1024)} %reshape.302) | copy-start | bytes 86020
  173.1 3.4 %copy-start.29 = (f32[1792]{0:T(1024)S(1)}, f32[1792]{0:T(1024)}, u32[]{:S(2)}) copy-start(f32[1792]{0:T(1024)} %get-tuple-element.58) | copy-start | bytes 21508
  173.1 3.4 %copy-start.38 = (f32[1536]{0:T(1024)S(1)}, f32[1536]{0:T(1024)}, u32[]{:S(2)}) copy-start(f32[1536]{0:T(1024)} %get-tuple-element.56) | copy-start | bytes 18436
  173.2 3.4 %copy-start.40 = (f32[24]{0:T(128)S(1)}, f32[24]{0:T(128)}, u32[]{:S(2)}) copy-start(f32[24]{0:T(128)} %reduce_sum.146) | copy-start | bytes 292
  173.2 3.4 %copy-start.44 = (f32[24]{0:T(128)S(1)}, f32[24]{0:T(128)}, u32[]{:S(2)}) copy-start(f32[24]{0:T(128)} %get-tuple-element.66) | copy-start | bytes 292
  173.2 4.1 %copy-start.33 = (f32[512]{0:T(512)S(1)}, f32[512]{0:T(512)}, u32[]{:S(2)}) copy-start(f32[512]{0:T(512)} %copy-done.32) | copy-start | bytes 6148
  173.2 4.1 %copy-start.17 = (bf16[512,768]{1,0:T(8,128)(2,1)S(1)}, bf16[512,768]{1,0:T(8,128)(2,1)}, u32[]{:S(2)}) copy-start(bf16[512,768]{1,0:T(8,128)(2,1)} %param.13) | copy-start | bytes 2359300
  (18 other events, 43.7 us)
